TPU v7x, 32 devices: a whole 2x2x4 slice. The times are simulated.
32 devices in a mesh: replica: 8 (over z, core), group: 4 (over y, x).
Axes of the slice: x: 2, y: 2, z: 4, core: 2. Of those that a mesh axis runs over, the one named last changes fastest.
Arguments:
- tokens: bfloat16 [4096, 2048], P(('replica', 'group')), may hold values from -6 to 6
- lengths: int32 [8], P('replica'), may hold values from 128 to 512, as said below
- exit_layers: int32 [4096], P(('replica', 'group')), may hold values from 7 to 20, as said below
- pre_gain: bfloat16 [2048], P('group'), may hold values from 0.099609375 to 1.8984375
- pre_shift: bfloat16 [2048], P('group'), may hold values from -3 to 3
- query_weight: bfloat16 [2048, 2048], P('group'), may hold values from -0.1875 to 0.1875
- query_bias: bfloat16 [2048], P('group'), may hold values from -3 to 3
- key_weight: bfloat16 [2048, 2048], P('group'), may hold values from -0.1875 to 0.1875
- value_weight: bfloat16 [2048, 2048], P('group'), may hold values from -0.125 to 0.125
- value_bias: bfloat16 [2048], P('group'), may hold values from -3 to 3
- out_weight: bfloat16 [2048, 2048], P('group'), may hold values from -0.5 to 0.5
- out_bias: bfloat16 [2048], P('group'), may hold values from -1.75 to 1.75
- mid_gain: bfloat16 [2048], P('group'), may hold values from 0.099609375 to 1.8984375
- mid_shift: bfloat16 [2048], P('group'), may hold values from -3 to 3
- up_weight: bfloat16 [2048, 8192], P(None, 'group'), may hold values from -0.125 to 0.125
- up_bias: bfloat16 [8192], P('group'), may hold values from -3 to 3
- down_weight: bfloat16 [8192, 2048], P('group'), may hold values from -0.0625 to 0.0625
- down_bias: bfloat16 [2048], P('group'), may hold values from -1.75 to 1.75
- cotangent: bfloat16 [4096, 2048], P(('replica', 'group')), may hold values from -6 to 6
Outputs:
- output: bfloat16 [4096, 2048], P(('replica', 'group'))
- token_grad: bfloat16 [4096, 2048], P(('replica', 'group'))
- pre_gain_grad: float32 [2048], P('group')
- pre_shift_grad: float32 [2048], P('group')
- query_weight_grad: float32 [2048, 2048], P('group')
- query_bias_grad: float32 [2048], P('group')
- key_weight_grad: float32 [2048, 2048], P('group')
- value_weight_grad: float32 [2048, 2048], P('group')
- value_bias_grad: float32 [2048], P('group')
- out_weight_grad: float32 [2048, 2048], P('group')
- out_bias_grad: float32 [2048], P('group')
- mid_gain_grad: float32 [2048], P('group')
- mid_shift_grad: float32 [2048], P('group')
- up_weight_grad: float32 [2048, 8192], P(None, 'group')
- up_bias_grad: float32 [8192], P('group')
- down_weight_grad: float32 [8192, 2048], P('group')
- down_bias_grad: float32 [2048], P('group')
Inputs may be any that keep to these rules, and one draw needn't show every extreme that they name: `lengths`: some sequence has length 512 and some other has length 128. Within each sequence, exit_layers never rise from one position to the next.
All inputs are finite; a program needn't handle non-finite values.
Results may differ from a plain program's by a relative error of at most 0.02.
Values may be sent and summed in bfloat16 or wider, within the bound.
No kernel may reach another device: no remote copies, remote signals or barrier semaphores. Data moves between devices by JAX's collectives and lax.ppermute only.
A program may use at most 640 MiB of HBM per device.

v0:
```python
import jax
import jax.numpy as jnp
from jax import lax
from jax.sharding import PartitionSpec as P

D = 2048
H = 32
HD = 64
LAYER = 12


def layer_norm(values):
    center = values - jnp.mean(values, -1, keepdims=True)
    spread = jnp.mean(center * center, -1, keepdims=True)
    factor = lax.rsqrt(spread + 1e-05)
    return (center * factor, factor)


def norm_back(grad, normal, factor):
    return factor * (
        grad
        - jnp.mean(grad, -1, keepdims=True)
        - normal * jnp.mean(grad * normal, -1, keepdims=True)
    )


def gelu(values):
    return (
        0.5
        * values
        * (1.0 + jnp.tanh(0.7978845608 * (values + 0.044715 * values * values * values)))
    )


def gelu_back(values, grad):
    inner = 0.7978845608 * (values + 0.044715 * values * values * values)
    tangent = jnp.tanh(inner)
    slope = 0.5 * (1.0 + tangent) + 0.5 * values * (1.0 - tangent * tangent) * 0.7978845608 * (
        1.0 + 3.0 * 0.044715 * values * values
    )
    return grad * slope


def split_heads(matrix):
    groups = max(1, H // 8)
    return matrix.reshape(matrix.shape[0], groups, H // groups, HD).transpose(1, 0, 2, 3)


def join_heads(heads):
    return heads.transpose(1, 0, 2, 3).reshape(heads.shape[1], D)


def score_block(query_group, key_group, allowed):
    scores = (
        jnp.einsum("qhd,khd->hqk", query_group, key_group, preferred_element_type=jnp.float32)
        * 0.125
    )
    return jnp.where(allowed[None], scores, -1e30)


def matmul(left, right):
    return jnp.dot(left, right, preferred_element_type=jnp.float32)


def column_sums(matrix):
    return jnp.sum(matrix.astype(jnp.float32), 0)


def shards(
    tokens,
    lengths,
    exit_layers,
    pre_gain,
    pre_shift,
    query_weight,
    query_bias,
    key_weight,
    value_weight,
    value_bias,
    out_weight,
    out_bias,
    mid_gain,
    mid_shift,
    up_weight,
    up_bias,
    down_weight,
    down_bias,
    cotangent,
):
    local_rows = tokens.shape[0]
    group_count = lax.axis_size("group")
    seq_rows = local_rows * group_count
    member = lax.axis_index("group")
    position = member * local_rows + jnp.arange(local_rows, dtype=jnp.int32)
    active = ((position < lengths[0]) & (exit_layers > LAYER)).astype(jnp.float32)[:, None]
    allowed = jnp.arange(seq_rows, dtype=jnp.int32)[None, :] <= position[:, None]
    (
        gain_one,
        shift_one,
        gain_two,
        shift_two,
        query_full,
        key_full,
        value_full,
        out_full,
        qbias_full,
        vbias_full,
        obias_full,
    ) = (
        lax.all_gather(pre_gain, "group", axis=0, tiled=True),
        lax.all_gather(pre_shift, "group", axis=0, tiled=True),
        lax.all_gather(mid_gain, "group", axis=0, tiled=True),
        lax.all_gather(mid_shift, "group", axis=0, tiled=True),
        lax.all_gather(query_weight, "group", axis=0, tiled=True),
        lax.all_gather(key_weight, "group", axis=0, tiled=True),
        lax.all_gather(value_weight, "group", axis=0, tiled=True),
        lax.all_gather(out_weight, "group", axis=0, tiled=True),
        lax.all_gather(query_bias, "group", axis=0, tiled=True),
        lax.all_gather(value_bias, "group", axis=0, tiled=True),
        lax.all_gather(out_bias, "group", axis=0, tiled=True),
    )
    inputs = tokens.astype(jnp.float32)
    normed_one, factor_one = layer_norm(inputs)
    attn_in = (normed_one * gain_one.astype(jnp.float32) + shift_one.astype(jnp.float32)).astype(
        jnp.bfloat16
    )
    queries = (matmul(attn_in, query_full) + qbias_full.astype(jnp.float32)).astype(jnp.bfloat16)
    keys_local = matmul(attn_in, key_full).astype(jnp.bfloat16)
    values_local = (matmul(attn_in, value_full) + vbias_full.astype(jnp.float32)).astype(
        jnp.bfloat16
    )
    keys_all, values_all = (
        lax.all_gather(keys_local, "group", axis=0, tiled=True),
        lax.all_gather(values_local, "group", axis=0, tiled=True),
    )
    query_heads = split_heads(queries)
    key_heads = split_heads(keys_all)
    value_heads = split_heads(values_all)

    def forward_group(operands):
        query_group, key_group, value_group = operands
        scores = score_block(query_group, key_group, allowed)
        top = jnp.max(scores, -1, keepdims=True)
        logsum = top + jnp.log(jnp.sum(jnp.exp(scores - top), -1, keepdims=True))
        weights = jnp.exp(scores - logsum).astype(jnp.bfloat16)
        context_part = jnp.einsum(
            "hqk,khd->qhd", weights, value_group, preferred_element_type=jnp.float32
        )
        return (context_part, logsum[..., 0])

    context_heads, logsums = lax.map(forward_group, (query_heads, key_heads, value_heads))
    context_low = join_heads(context_heads).astype(jnp.bfloat16)
    attn_out = matmul(context_low, out_full) + obias_full.astype(jnp.float32)
    hidden = inputs + active * attn_out
    normed_two, factor_two = layer_norm(hidden)
    ffn_in = (normed_two * gain_two.astype(jnp.float32) + shift_two.astype(jnp.float32)).astype(
        jnp.bfloat16
    )
    up_full, upbias_full, down_full, downbias_full = (
        lax.all_gather(up_weight, "group", axis=1, tiled=True),
        lax.all_gather(up_bias, "group", axis=0, tiled=True),
        lax.all_gather(down_weight, "group", axis=0, tiled=True),
        lax.all_gather(down_bias, "group", axis=0, tiled=True),
    )
    pre_act = matmul(ffn_in, up_full) + upbias_full.astype(jnp.float32)
    act_low = gelu(pre_act).astype(jnp.bfloat16)
    branch = matmul(act_low, down_full) + downbias_full.astype(jnp.float32)
    output = (hidden + active * branch).astype(jnp.bfloat16)
    first_gain, second_gain, query_back, key_back, value_back, out_back = (
        lax.all_gather(pre_gain, "group", axis=0, tiled=True),
        lax.all_gather(mid_gain, "group", axis=0, tiled=True),
        lax.all_gather(query_weight, "group", axis=0, tiled=True),
        lax.all_gather(key_weight, "group", axis=0, tiled=True),
        lax.all_gather(value_weight, "group", axis=0, tiled=True),
        lax.all_gather(out_weight, "group", axis=0, tiled=True),
    )
    grad_out = cotangent.astype(jnp.float32)
    branch_grad = (active * grad_out).astype(jnp.bfloat16)
    up_back, down_back = (
        lax.all_gather(up_weight, "group", axis=1, tiled=True),
        lax.all_gather(down_weight, "group", axis=0, tiled=True),
    )
    act_grad = matmul(branch_grad, down_back.T)
    pre_grad = gelu_back(pre_act, act_grad).astype(jnp.bfloat16)
    ffn_in_grad = matmul(pre_grad, up_back.T)
    up_grad, up_bias_grad, down_grad, down_bias_grad = (
        lax.psum_scatter(
            matmul(ffn_in.T, pre_grad).astype(jnp.bfloat16),
            "group",
            scatter_dimension=1,
            tiled=True,
        ).astype(jnp.float32),
        lax.psum_scatter(
            column_sums(pre_grad).astype(jnp.bfloat16), "group", scatter_dimension=0, tiled=True
        ).astype(jnp.float32),
        lax.psum_scatter(
            matmul(act_low.T, branch_grad).astype(jnp.bfloat16),
            "group",
            scatter_dimension=0,
            tiled=True,
        ).astype(jnp.float32),
        lax.psum_scatter(
            column_sums(branch_grad).astype(jnp.bfloat16), "group", scatter_dimension=0, tiled=True
        ).astype(jnp.float32),
    )
    mid_gain_part = jnp.sum(ffn_in_grad * normed_two, 0)
    mid_shift_part = jnp.sum(ffn_in_grad, 0)
    hidden_grad = grad_out + norm_back(
        ffn_in_grad * second_gain.astype(jnp.float32), normed_two, factor_two
    )
    attn_grad = (active * hidden_grad).astype(jnp.bfloat16)
    context_grad = matmul(attn_grad, out_back.T).astype(jnp.bfloat16)
    out_bias_part = column_sums(attn_grad)

    def backward_group(operands):
        query_group, key_group, value_group, grad_group, logsum_group = operands
        scores = score_block(query_group, key_group, allowed)
        probs = jnp.exp(scores - logsum_group[..., None])
        probs_grad = jnp.einsum(
            "qhd,khd->hqk", grad_group, value_group, preferred_element_type=jnp.float32
        )
        delta = jnp.sum(probs * probs_grad, -1, keepdims=True)
        score_grad = (probs * (probs_grad - delta)).astype(jnp.bfloat16)
        query_part = (
            jnp.einsum("hqk,khd->qhd", score_grad, key_group, preferred_element_type=jnp.float32)
            * 0.125
        )
        key_part = (
            jnp.einsum("hqk,qhd->khd", score_grad, query_group, preferred_element_type=jnp.float32)
            * 0.125
        )
        value_part = jnp.einsum(
            "hqk,qhd->khd",
            probs.astype(jnp.bfloat16),
            grad_group,
            preferred_element_type=jnp.float32,
        )
        return (query_part, key_part, value_part)

    query_parts, key_parts, value_parts = lax.map(
        backward_group, (query_heads, key_heads, value_heads, split_heads(context_grad), logsums)
    )
    query_grad = join_heads(query_parts).astype(jnp.bfloat16)
    key_sum, value_sum = (
        lax.psum_scatter(
            join_heads(key_parts).astype(jnp.bfloat16), "group", scatter_dimension=0, tiled=True
        ).astype(jnp.float32),
        lax.psum_scatter(
            join_heads(value_parts).astype(jnp.bfloat16), "group", scatter_dimension=0, tiled=True
        ).astype(jnp.float32),
    )
    key_grad = key_sum.astype(jnp.bfloat16)
    value_grad = value_sum.astype(jnp.bfloat16)
    in_grad = (
        matmul(query_grad, query_back.T)
        + matmul(key_grad, key_back.T)
        + matmul(value_grad, value_back.T)
    )
    pre_gain_part = jnp.sum(in_grad * normed_one, 0)
    pre_shift_part = jnp.sum(in_grad, 0)
    token_grad = (
        hidden_grad + norm_back(in_grad * first_gain.astype(jnp.float32), normed_one, factor_one)
    ).astype(jnp.bfloat16)
    (
        pre_gain_grad,
        pre_shift_grad,
        mid_gain_grad,
        mid_shift_grad,
        query_wgrad,
        key_wgrad,
        value_wgrad,
        out_wgrad,
        query_bgrad,
        value_bgrad,
        out_bgrad,
    ) = (
        lax.psum_scatter(
            pre_gain_part.astype(jnp.bfloat16), "group", scatter_dimension=0, tiled=True
        ).astype(jnp.float32),
        lax.psum_scatter(
            pre_shift_part.astype(jnp.bfloat16), "group", scatter_dimension=0, tiled=True
        ).astype(jnp.float32),
        lax.psum_scatter(
            mid_gain_part.astype(jnp.bfloat16), "group", scatter_dimension=0, tiled=True
        ).astype(jnp.float32),
        lax.psum_scatter(
            mid_shift_part.astype(jnp.bfloat16), "group", scatter_dimension=0, tiled=True
        ).astype(jnp.float32),
        lax.psum_scatter(
            matmul(attn_in.T, query_grad).astype(jnp.bfloat16),
            "group",
            scatter_dimension=0,
            tiled=True,
        ).astype(jnp.float32),
        lax.psum_scatter(
            matmul(attn_in.T, key_grad).astype(jnp.bfloat16),
            "group",
            scatter_dimension=0,
            tiled=True,
        ).astype(jnp.float32),
        lax.psum_scatter(
            matmul(attn_in.T, value_grad).astype(jnp.bfloat16),
            "group",
            scatter_dimension=0,
            tiled=True,
        ).astype(jnp.float32),
        lax.psum_scatter(
            matmul(context_low.T, attn_grad).astype(jnp.bfloat16),
            "group",
            scatter_dimension=0,
            tiled=True,
        ).astype(jnp.float32),
        lax.psum_scatter(
            column_sums(query_grad).astype(jnp.bfloat16), "group", scatter_dimension=0, tiled=True
        ).astype(jnp.float32),
        lax.psum_scatter(
            column_sums(value_grad).astype(jnp.bfloat16), "group", scatter_dimension=0, tiled=True
        ).astype(jnp.float32),
        lax.psum_scatter(
            out_bias_part.astype(jnp.bfloat16), "group", scatter_dimension=0, tiled=True
        ).astype(jnp.float32),
    )
    totals = (
        lax.psum(pre_gain_grad.astype(jnp.bfloat16), "replica").astype(jnp.float32),
        lax.psum(pre_shift_grad.astype(jnp.bfloat16), "replica").astype(jnp.float32),
        lax.psum(query_wgrad.astype(jnp.bfloat16), "replica").astype(jnp.float32),
        lax.psum(query_bgrad.astype(jnp.bfloat16), "replica").astype(jnp.float32),
        lax.psum(key_wgrad.astype(jnp.bfloat16), "replica").astype(jnp.float32),
        lax.psum(value_wgrad.astype(jnp.bfloat16), "replica").astype(jnp.float32),
        lax.psum(value_bgrad.astype(jnp.bfloat16), "replica").astype(jnp.float32),
        lax.psum(out_wgrad.astype(jnp.bfloat16), "replica").astype(jnp.float32),
        lax.psum(out_bgrad.astype(jnp.bfloat16), "replica").astype(jnp.float32),
        lax.psum(mid_gain_grad.astype(jnp.bfloat16), "replica").astype(jnp.float32),
        lax.psum(mid_shift_grad.astype(jnp.bfloat16), "replica").astype(jnp.float32),
        lax.psum(up_grad.astype(jnp.bfloat16), "replica").astype(jnp.float32),
        lax.psum(up_bias_grad.astype(jnp.bfloat16), "replica").astype(jnp.float32),
        lax.psum(down_grad.astype(jnp.bfloat16), "replica").astype(jnp.float32),
        lax.psum(down_bias_grad.astype(jnp.bfloat16), "replica").astype(jnp.float32),
    )
    return (
        output,
        token_grad,
        totals[0],
        totals[1],
        totals[2],
        totals[3],
        totals[4],
        totals[5],
        totals[6],
        totals[7],
        totals[8],
        totals[9],
        totals[10],
        totals[11],
        totals[12],
        totals[13],
        totals[14],
    )


def solution(mesh):
    return jax.shard_map(
        shards,
        mesh=mesh,
        in_specs=(
            P(("replica", "group"), None),
            P("replica"),
            P(("replica", "group")),
            P("group"),
            P("group"),
            P("group", None),
            P("group"),
            P("group", None),
            P("group", None),
            P("group"),
            P("group", None),
            P("group"),
            P("group"),
            P("group"),
            P(None, "group"),
            P("group"),
            P("group", None),
            P("group"),
            P(("replica", "group"), None),
        ),
        out_specs=(
            P(("replica", "group"), None),
            P(("replica", "group"), None),
            P("group"),
            P("group"),
            P("group", None),
            P("group"),
            P("group", None),
            P("group", None),
            P("group"),
            P("group", None),
            P("group"),
            P("group"),
            P("group"),
            P(None, "group"),
            P("group"),
            P("group", None),
            P("group"),
        ),
        check_vma=False,
    )
```

profile of v0, /device:TPU:0, one launch (start us, length us, event | category | flops | bytes accessed | tf_op | source)
XLA Modules:
  0.0 2687.4 jit_solution(7998907598796842740)
XLA Ops:
  34.8 65.6 %all-gather.17.cloned.1.call-done = bf16[2048,2048]{1,0:T(8,128)(2,1)} async-done(((bf16[512,2048]{1,0:T(8,128)(2,1)}), bf16[2048,2048]{1,0:T(8,128)(2,1)}) %all-gather.17.cloned.1.call-update) | async-done | bytes 8388624 | tf_op jit(solution)/shard_map/all_gather | solution.py:116
  105.9 83.9 %all-gather.23.cloned.1.call-done = bf16[2048,2048]{1,0:T(8,128)(2,1)} async-done(((bf16[512,2048]{1,0:T(8,128)(2,1)}), bf16[2048,2048]{1,0:T(8,128)(2,1)}) %all-gather.23.cloned.1.call-update) | async-done | bytes 8388624 | tf_op jit(solution)/shard_map/all_gather | solution.py:115
  237.1 42.5 %all-gather.21.cloned.1.call-done = bf16[2048,2048]{1,0:T(8,128)(2,1)} async-done(((bf16[512,2048]{1,0:T(8,128)(2,1)}), bf16[2048,2048]{1,0:T(8,128)(2,1)}) %all-gather.21.cloned.1.call-update) | async-done | bytes 8388624 | tf_op jit(solution)/shard_map/all_gather | solution.py:114
  284.6 32.6 %all-gather.19.cloned.1.call-done = bf16[512,2048]{1,0:T(8,128)(2,1)} async-done(((bf16[128,2048]{1,0:T(8,128)(2,1)}), bf16[512,2048]{1,0:T(8,128)(2,1)}) %all-gather.19.cloned.1.call-update) | async-done | bytes 2097168 | tf_op jit(solution)/shard_map/all_gather | solution.py:134
  321.3 33.5 %all-gather.25.cloned.1.call-done = bf16[512,2048]{1,0:T(8,128)(2,1)} async-done(((bf16[128,2048]{1,0:T(8,128)(2,1)}), bf16[512,2048]{1,0:T(8,128)(2,1)}) %all-gather.25.cloned.1.call-update) | async-done | bytes 2097168 | tf_op jit(solution)/shard_map/all_gather | solution.py:133
  374.4 69.8 %all-gather.27.cloned.1.call-done = bf16[2048,2048]{1,0:T(8,128)(2,1)} async-done(((bf16[512,2048]{1,0:T(8,128)(2,1)}), bf16[2048,2048]{1,0:T(8,128)(2,1)}) %all-gather.27.cloned.1.call-update) | async-done | bytes 8388624 | tf_op jit(solution)/shard_map/all_gather | solution.py:117
  450.3 292.9 %all-gather.29.cloned.1.call-done = bf16[2048,8192]{1,0:T(8,128)(2,1)} async-done(((bf16[2048,2048]{1,0:T(8,128)(2,1)}), bf16[2048,8192]{1,0:T(8,128)(2,1)}) %all-gather.29.cloned.1.call-update) | async-done | bytes 33554448 | tf_op jit(solution)/shard_map/all_gather | solution.py:160
  743.3 20.8 convolution_add_fusion
  764.0 278.3 %all-gather.31.cloned.1.call-done = bf16[8192,2048]{1,0:T(8,128)(2,1)} async-done(((bf16[2048,2048]{1,0:T(8,128)(2,1)}), bf16[8192,2048]{1,0:T(8,128)(2,1)}) %all-gather.31.cloned.1.call-update) | async-done | bytes 33554448 | tf_op jit(solution)/shard_map/all_gather | solution.py:162
  1042.3 18.8 fusion.81
  1061.2 19.7 multiply_reduce_fusion.1
  1095.0 31.3 %while.29 = (s32[]{:T(128)}, bf16[4,128,8,64]{1,3,2,0:T(8,128)(2,1)}, bf16[4,512,8,64]{1,3,2,0:T(8,128)(2,1)}, bf16[4,512,8,64]{1,3,2,0:T(8,128)(2,1)}, bf16[4,5...) while((s32[]{:T(128)}, ...), condition=%wide.region_12.13_spmd.clone, body=%wide.region_10.12_spmd.clone.sunk | while | flops 340655104 | bytes 58091296 | solution.py:240
  1147.0 18.6 reduce-scatter.25.cloned.1.call-done
  1172.5 31.9 %reduce-scatter.27.cloned.1.call-done = bf16[128,2048]{1,0:T(8,128)(2,1)} async-done(((bf16[512,2048]{1,0:T(8,128)(2,1)}), bf16[128,2048]{1,0:T(8,128)(2,1)}) %reduce-scatter.27.cloned.1.call-update) | async-done | bytes 524304
  1229.1 16.6 convolution_convert_fusion.1
  1245.8 48.8 %reduce-scatter.15.cloned.1.call-done = bf16[512,2048]{1,0:T(8,128)(2,1)} async-done(((bf16[2048,2048]{1,0:T(8,128)(2,1)}), bf16[512,2048]{1,0:T(8,128)(2,1)}) %reduce-scatter.15.cloned.1.call-update) | async-done | bytes 2097168 | tf_op jit(solution)/shard_map/reduce_scatter | solution.py:289
  1294.5 89.6 %reduce-scatter.21.cloned.1.call-done = bf16[512,2048]{1,0:T(8,128)(2,1)} async-done(((bf16[2048,2048]{1,0:T(8,128)(2,1)}), bf16[512,2048]{1,0:T(8,128)(2,1)}) %reduce-scatter.21.cloned.1.call-update) | async-done | bytes 2097168 | tf_op jit(solution)/shard_map/reduce_scatter | solution.py:307
  1384.2 90.1 %reduce-scatter.17.cloned.1.call-done = bf16[512,2048]{1,0:T(8,128)(2,1)} async-done(((bf16[2048,2048]{1,0:T(8,128)(2,1)}), bf16[512,2048]{1,0:T(8,128)(2,1)}) %reduce-scatter.17.cloned.1.call-update) | async-done | bytes 2097168 | tf_op jit(solution)/shard_map/reduce_scatter | solution.py:295
  1474.2 89.6 %reduce-scatter.19.cloned.1.call-done = bf16[512,2048]{1,0:T(8,128)(2,1)} async-done(((bf16[2048,2048]{1,0:T(8,128)(2,1)}), bf16[512,2048]{1,0:T(8,128)(2,1)}) %reduce-scatter.19.cloned.1.call-update) | async-done | bytes 2097168 | tf_op jit(solution)/shard_map/reduce_scatter | solution.py:301
  1563.9 291.6 %reduce-scatter.23.cloned.1.call-done = bf16[2048,2048]{1,0:T(8,128)(2,1)} async-done(((bf16[2048,8192]{1,0:T(8,128)(2,1)}), bf16[2048,2048]{1,0:T(8,128)(2,1)}) %reduce-scatter.23.cloned.1.call-update) | async-done | bytes 8388624 | tf_op jit(solution)/shard_map/reduce_scatter | solution.py:187
  1855.5 291.9 %reduce-scatter.29.cloned.1.call-done = bf16[2048,2048]{1,0:T(8,128)(2,1)} async-done(((bf16[8192,2048]{1,0:T(8,128)(2,1)}), bf16[2048,2048]{1,0:T(8,128)(2,1)}) %reduce-scatter.29.cloned.1.call-update) | async-done | bytes 8388624
  2164.9 18.0 fusion.52
  2213.1 28.0 %all-reduce.10 = (bf16[512]{0:T(512)(128)(2,1)S(1)}, bf16[512]{0:T(512)(128)(2,1)S(1)}, bf16[512]{0:T(512)(128)(2,1)S(1)}, bf16[512]{0:T(512)(128)(2,1)S(1)}, bf...) all-reduce(bf16[512]{0:T(512)(128)(2,1)S(1)} %dynamic-slice.1, ...), channel_id=1, replica_groups=mesh['replica'=8,'group'=4] {'replica'}, use_global_device_ids=true, to_apply=%region_19.20 | all-reduce | flops 6144 | bytes 24576 | tf_op jit(solution)/shard_map/psum | solution.py:324
  2247.6 397.6 %all-reduce.15.cloned.1.call-done = (bf16[512,2048]{1,0:T(8,128)(2,1)}, bf16[512,2048]{1,0:T(8,128)(2,1)}, bf16[512,2048]{1,0:T(8,128)(2,1)}, bf16[512,2048]{1,0...) async-done(((bf16[512,2048]{1,0:T(8,128)(2,1)}, bf16[512,2048]{1,0:T(8,128)(2,1)}, bf16[512,2048]{1,0:T(8,128)(2,1)}, bf16[512,2048]{1,0:T(8,128)(2,1)}, ...) | async-done | bytes 25165840 | tf_op jit(solution)/shard_map/psum | solution.py:326
  (292 shorter events, 315.1 us)
Async XLA Ops:
  7.2 19.9 copy-start.24
  7.2 27.1 %copy-start = (bf16[128,2048]{1,0:T(8,128)(2,1)S(1)}, bf16[128,2048]{1,0:T(8,128)(2,1)}, u32[]{:S(2)}) copy-start(bf16[128,2048]{1,0:T(8,128)(2,1)} %param.23) | copy-start | bytes 1572868
  7.2 93.1 %all-gather.17.cloned.1.call-start = ((), (), s32[]{:S(2)}) async-start(), calls=%async_computation.8 | async-start | bytes 10485760 | tf_op jit(solution)/shard_map/all_gather | solution.py:116
  8.0 181.9 %all-gather.23.cloned.1.call-start = ((), (), s32[]{:S(2)}) async-start(), calls=%async_computation.11 | async-start | bytes 10485760 | tf_op jit(solution)/shard_map/all_gather | solution.py:115
  8.7 270.9 %all-gather.21.cloned.1.call-start = ((), (), s32[]{:S(2)}) async-start(), calls=%async_computation.10 | async-start | bytes 10485760 | tf_op jit(solution)/shard_map/all_gather | solution.py:114
  9.4 307.7 %all-gather.19.cloned.1.call-start = ((), (), s32[]{:S(2)}) async-start(), calls=%async_computation.9 | async-start | bytes 2621440 | tf_op jit(solution)/shard_map/all_gather | solution.py:134
  105.9 248.9 %all-gather.25.cloned.1.call-start = ((), (), s32[]{:S(2)}) async-start(), calls=%async_computation.12 | async-start | bytes 2621440 | tf_op jit(solution)/shard_map/all_gather | solution.py:133
  195.4 248.8 %all-gather.27.cloned.1.call-start = ((), (), s32[]{:S(2)}) async-start(), calls=%async_computation.13 | async-start | bytes 10485760 | tf_op jit(solution)/shard_map/all_gather | solution.py:117
  195.9 547.3 %all-gather.29.cloned.1.call-start = ((), (), s32[]{:S(2)}) async-start(), calls=%async_computation.14 | async-start | bytes 41943040 | tf_op jit(solution)/shard_map/all_gather | solution.py:160
  196.7 25.1 copy-start.27
  196.7 32.2 %copy-start.28 = (bf16[512]{0:T(512)(128)(2,1)S(1)}, bf16[512]{0:T(512)(128)(2,1)}, u32[]{:S(2)}) copy-start(bf16[512]{0:T(512)(128)(2,1)} %param.35) | copy-start | bytes 3076
  196.7 40.3 %copy-start.30 = (s32[128]{0:T(128)S(1)}, s32[128]{0:T(128)}, u32[]{:S(2)}) copy-start(s32[128]{0:T(128)} %param.25) | copy-start | bytes 1540
  196.8 845.6 %all-gather.31.cloned.1.call-start = ((), (), s32[]{:S(2)}) async-start(), calls=%async_computation.15 | async-start | bytes 41943040 | tf_op jit(solution)/shard_map/all_gather | solution.py:162
  197.5 968.0 %reduce-scatter.25.cloned.1.call-start = ((), (), s32[]{:S(2)}) async-start(), calls=%async_computation.21 | async-start | bytes 2621440
  1130.2 74.2 %reduce-scatter.27.cloned.1.call-start = ((), (), s32[]{:S(2)}) async-start(), calls=%async_computation.22 | async-start | bytes 2621440
  1134.2 160.3 %reduce-scatter.15.cloned.1.call-start = ((), (), s32[]{:S(2)}) async-start(), calls=%async_computation.16 | async-start | bytes 10485760 | tf_op jit(solution)/shard_map/reduce_scatter | solution.py:289
  1140.2 244.0 %reduce-scatter.21.cloned.1.call-start = ((), (), s32[]{:S(2)}) async-start(), calls=%async_computation.19 | async-start | bytes 10485760 | tf_op jit(solution)/shard_map/reduce_scatter | solution.py:307
  1146.9 327.3 %reduce-scatter.17.cloned.1.call-start = ((), (), s32[]{:S(2)}) async-start(), calls=%async_computation.17 | async-start | bytes 10485760 | tf_op jit(solution)/shard_map/reduce_scatter | solution.py:295
  1172.5 391.4 %reduce-scatter.19.cloned.1.call-start = ((), (), s32[]{:S(2)}) async-start(), calls=%async_computation.18 | async-start | bytes 10485760 | tf_op jit(solution)/shard_map/reduce_scatter | solution.py:301
  1211.2 644.3 %reduce-scatter.23.cloned.1.call-start = ((), (), s32[]{:S(2)}) async-start(), calls=%async_computation.20 | async-start | bytes 41943040 | tf_op jit(solution)/shard_map/reduce_scatter | solution.py:187
  1228.1 919.2 %reduce-scatter.29.cloned.1.call-start = ((), (), s32[]{:S(2)}) async-start(), calls=%async_computation.23 | async-start | bytes 41943040
  1245.7 1399.5 %all-reduce.15.cloned.1.call-start = ((), (), s32[]{:S(2)}) async-start(), calls=%async_computation.24 | async-start | bytes 50331648 | tf_op jit(solution)/shard_map/psum | solution.py:326
  2164.8 18.1 copy-start.9
  2189.5 56.9 %copy-start.12 = (f32[128,2048]{1,0:T(8,128)S(1)}, f32[128,2048]{1,0:T(8,128)}, u32[]{:S(2)}) copy-start(f32[128,2048]{1,0:T(8,128)} %get-tuple-element.224) | copy-start | bytes 3145732
  (49 other events, 125.0 us)
Sparse Core Ops, SparseCore 0:
  9.9 90.3 all-gather.16
  102.2 87.5 all-gather.22
  191.7 87.8 all-gather.20
  281.8 35.3 all-gather.18
  319.5 35.2 all-gather.24
  356.5 87.5 all-gather.26
  446.0 297.2 all-gather.28
  745.1 297.2 all-gather.30
  1130.3 35.1 reduce-scatter.24
  1169.2 35.1 reduce-scatter.26
  1208.1 86.3 reduce-scatter.14
  1297.7 86.3 reduce-scatter.20
  1387.8 86.3 reduce-scatter.16
  1477.4 86.3 reduce-scatter.18
  1566.8 288.6 reduce-scatter.22
  1858.7 288.6 reduce-scatter.28
  2150.5 494.6 all-reduce.14
where the time goes:
time: 2690 us
  waiting for transfers between devices  2250 us (84%)
  matrix products  210 us (8%)
  blocking collectives  116 us (4%)
  other arithmetic  50.9 us (2%)
  local copies, waits for them, and re-layouts  39.5 us (1%)
    psum x1, waiting for transfers between devices, shards(): lax.psum(query_wgrad.astype(jnp.bfloat16), 'replica').astype(jnp.float32)  398 us
    unnamed x20, waiting for transfers between devices  346 us
    all_gather x1, waiting for transfers between devices, shards(): lax.all_gather(up_weight, 'group', axis=1, tiled=True)  293 us
    reduce_scatter x1, waiting for transfers between devices, shards(): lax.psum_scatter(matmul(ffn_in.T, pre_grad).astype(jnp.bfloat16), 'group'...  292 us
    all_gather x1, waiting for transfers between devices, shards(): lax.all_gather(down_weight, 'group', axis=0, tiled=True)  278 us
    dot_general x18, matrix products, matmul(): return jnp.dot(left, right, preferred_element_type=jnp.float32)  182 us
    reduce_scatter x1, waiting for transfers between devices, shards(): lax.psum_scatter(matmul(attn_in.T, key_grad).astype(jnp.bfloat16), 'group...  90.1 us
    reduce_scatter x1, waiting for transfers between devices, shards(): lax.psum_scatter(matmul(attn_in.T, value_grad).astype(jnp.bfloat16), 'gro...  89.6 us
  transfers between devices with their start and end apart: 17, of which 17 were waited for; matrix products, arithmetic and copies ran while one was open for 6% of the time, Pallas kernels for 0%

commit v1 on v0

--- a/solution.py
+++ b/solution.py
@@ -114,7 +114,9 @@
         lax.all_gather(query_weight, "group", axis=0, tiled=True),
         lax.all_gather(key_weight, "group", axis=0, tiled=True),
         lax.all_gather(value_weight, "group", axis=0, tiled=True),
-        lax.all_gather(out_weight, "group", axis=0, tiled=True),
+        jnp.concatenate(
+            lax.all_to_all(jnp.stack([out_weight] * lax.axis_size("group")), "group", 0, 0), axis=0
+        ),
         lax.all_gather(query_bias, "group", axis=0, tiled=True),
         lax.all_gather(value_bias, "group", axis=0, tiled=True),
         lax.all_gather(out_bias, "group", axis=0, tiled=True),

time: 2690 us -> 2730 us (1.015)
  blocking collectives: 116 us -> 240 us
  waiting for transfers between devices: 2250 us -> 2150 us
    all_gather x1, blocking collectives: 8.03 us -> 132 us  [shards(): lax.all_gather(out_bias, 'group', axis=0, tiled=True)]
    all_gather x1, waiting for transfers between devices: 42.5 us -> 0.02 us  [shards(): lax.all_gather(query_weight, 'group', axis=0, tiled=True)]
  transfers between devices with their start and end apart: 17 -> 18, of which waited for: 17 -> 16; matrix products, arithmetic and copies ran while one was open for 6% -> 8% of each run, Pallas kernels for 0% -> 0%
where the time goes in v1:
time: 2730 us
  waiting for transfers between devices  2150 us (79%)
  blocking collectives  240 us (9%)
  matrix products  214 us (8%)
  other arithmetic  51 us (2%)
  local copies, waits for them, and re-layouts  44.9 us (2%)
    psum x1, waiting for transfers between devices, shards(): lax.psum(query_wgrad.astype(jnp.bfloat16), 'replica').astype(jnp.float32)  398 us
    unnamed x20, waiting for transfers between devices  347 us
    reduce_scatter x1, waiting for transfers between devices, shards(): lax.psum_scatter(matmul(ffn_in.T, pre_grad).astype(jnp.bfloat16), 'group'...  292 us
    all_gather x1, waiting for transfers between devices, shards(): lax.all_gather(down_weight, 'group', axis=0, tiled=True)  278 us
    all_gather x1, waiting for transfers between devices, shards(): lax.all_gather(up_weight, 'group', axis=1, tiled=True)  271 us
    dot_general x18, matrix products, matmul(): return jnp.dot(left, right, preferred_element_type=jnp.float32)  186 us
    all_gather x1, blocking collectives, shards(): lax.all_gather(out_bias, 'group', axis=0, tiled=True)  132 us
    reduce_scatter x1, waiting for transfers between devices, shards(): lax.psum_scatter(matmul(attn_in.T, key_grad).astype(jnp.bfloat16), 'group...  90 us
  transfers between devices with their start and end apart: 18, of which 16 were waited for; matrix products, arithmetic and copies ran while one was open for 8% of the time, Pallas kernels for 0%

profile of v1, /device:TPU:0, one launch (start us, length us, event | category | flops | bytes accessed | tf_op | source)
XLA Modules:
  0.0 2727.3 jit_solution(519952414104864720)
XLA Ops:
  34.8 65.6 %all-gather.17.cloned.1.call-done = bf16[2048,2048]{1,0:T(8,128)(2,1)} async-done(((bf16[512,2048]{1,0:T(8,128)(2,1)}), bf16[2048,2048]{1,0:T(8,128)(2,1)}) %all-gather.17.cloned.1.call-update) | async-done | bytes 8388624 | tf_op jit(solution)/shard_map/all_gather | solution.py:116
  105.9 83.9 %all-gather.23.cloned.1.call-done = bf16[2048,2048]{1,0:T(8,128)(2,1)} async-done(((bf16[512,2048]{1,0:T(8,128)(2,1)}), bf16[2048,2048]{1,0:T(8,128)(2,1)}) %all-gather.23.cloned.1.call-update) | async-done | bytes 8388624 | tf_op jit(solution)/shard_map/all_gather | solution.py:115
  209.5 132.0 %all-gather.4 = bf16[4,1,512]{2,1,0:T(2,128)(2,1)S(1)} all-gather(bf16[1,1,512]{2,1,0:T(2,128)(2,1)S(1)} %reshape.159), channel_id=1, replica_groups=mesh['replica'=8,'group'=4] {'group'}, dimensions={0}, use_global_device_ids=true | all-gather | bytes 5120 | tf_op jit(solution)/shard_map/all_gather | solution.py:122
  377.9 21.5 all-gather.19.cloned.1.call-done
  403.6 33.5 %all-gather.25.cloned.1.call-done = bf16[512,2048]{1,0:T(8,128)(2,1)} async-done(((bf16[128,2048]{1,0:T(8,128)(2,1)}), bf16[512,2048]{1,0:T(8,128)(2,1)}) %all-gather.25.cloned.1.call-update) | async-done | bytes 2097168 | tf_op jit(solution)/shard_map/all_gather | solution.py:135
  465.4 270.6 %all-gather.27.cloned.1.call-done = bf16[2048,8192]{1,0:T(8,128)(2,1)} async-done(((bf16[2048,2048]{1,0:T(8,128)(2,1)}), bf16[2048,8192]{1,0:T(8,128)(2,1)}) %all-gather.27.cloned.1.call-update) | async-done | bytes 33554448 | tf_op jit(solution)/shard_map/all_gather | solution.py:162
  736.0 20.8 convolution_add_fusion
  756.8 278.3 %all-gather.29.cloned.1.call-done = bf16[8192,2048]{1,0:T(8,128)(2,1)} async-done(((bf16[2048,2048]{1,0:T(8,128)(2,1)}), bf16[8192,2048]{1,0:T(8,128)(2,1)}) %all-gather.29.cloned.1.call-update) | async-done | bytes 33554448 | tf_op jit(solution)/shard_map/all_gather | solution.py:164
  1035.1 20.4 fusion.81
  1055.5 19.7 multiply_reduce_fusion.1
  1078.7 45.9 %all-gather.31.cloned.1.call-done = bf16[2048,2048]{1,0:T(8,128)(2,1)} async-done(((bf16[512,2048]{1,0:T(8,128)(2,1)}), bf16[2048,2048]{1,0:T(8,128)(2,1)}) %all-gather.31.cloned.1.call-update) | async-done | bytes 8388624 | tf_op jit(solution)/shard_map/all_gather | solution.py:177
  1134.8 31.3 %while.29 = (s32[]{:T(128)}, bf16[4,128,8,64]{1,3,2,0:T(8,128)(2,1)}, bf16[4,512,8,64]{1,3,2,0:T(8,128)(2,1)}, bf16[4,512,8,64]{1,3,2,0:T(8,128)(2,1)}, bf16[4,5...) while((s32[]{:T(128)}, ...), condition=%wide.region_12.13_spmd.clone, body=%wide.region_10.12_spmd.clone.sunk | while | flops 340655104 | bytes 58091296 | solution.py:242
  1186.8 18.6 reduce-scatter.25.cloned.1.call-done
  1212.4 31.9 %reduce-scatter.27.cloned.1.call-done = bf16[128,2048]{1,0:T(8,128)(2,1)} async-done(((bf16[512,2048]{1,0:T(8,128)(2,1)}), bf16[128,2048]{1,0:T(8,128)(2,1)}) %reduce-scatter.27.cloned.1.call-update) | async-done | bytes 524304
  1269.0 16.5 convolution_convert_fusion.1
  1285.6 48.8 %reduce-scatter.15.cloned.1.call-done = bf16[512,2048]{1,0:T(8,128)(2,1)} async-done(((bf16[2048,2048]{1,0:T(8,128)(2,1)}), bf16[512,2048]{1,0:T(8,128)(2,1)}) %reduce-scatter.15.cloned.1.call-update) | async-done | bytes 2097168 | tf_op jit(solution)/shard_map/reduce_scatter | solution.py:291
  1334.3 89.7 %reduce-scatter.21.cloned.1.call-done = bf16[512,2048]{1,0:T(8,128)(2,1)} async-done(((bf16[2048,2048]{1,0:T(8,128)(2,1)}), bf16[512,2048]{1,0:T(8,128)(2,1)}) %reduce-scatter.21.cloned.1.call-update) | async-done | bytes 2097168 | tf_op jit(solution)/shard_map/reduce_scatter | solution.py:309
  1424.0 90.0 %reduce-scatter.17.cloned.1.call-done = bf16[512,2048]{1,0:T(8,128)(2,1)} async-done(((bf16[2048,2048]{1,0:T(8,128)(2,1)}), bf16[512,2048]{1,0:T(8,128)(2,1)}) %reduce-scatter.17.cloned.1.call-update) | async-done | bytes 2097168 | tf_op jit(solution)/shard_map/reduce_scatter | solution.py:297
  1514.0 89.7 %reduce-scatter.19.cloned.1.call-done = bf16[512,2048]{1,0:T(8,128)(2,1)} async-done(((bf16[2048,2048]{1,0:T(8,128)(2,1)}), bf16[512,2048]{1,0:T(8,128)(2,1)}) %reduce-scatter.19.cloned.1.call-update) | async-done | bytes 2097168 | tf_op jit(solution)/shard_map/reduce_scatter | solution.py:303
  1603.7 291.6 %reduce-scatter.23.cloned.1.call-done = bf16[2048,2048]{1,0:T(8,128)(2,1)} async-done(((bf16[2048,8192]{1,0:T(8,128)(2,1)}), bf16[2048,2048]{1,0:T(8,128)(2,1)}) %reduce-scatter.23.cloned.1.call-update) | async-done | bytes 8388624 | tf_op jit(solution)/shard_map/reduce_scatter | solution.py:189
  1895.3 291.9 %reduce-scatter.29.cloned.1.call-done = bf16[2048,2048]{1,0:T(8,128)(2,1)} async-done(((bf16[8192,2048]{1,0:T(8,128)(2,1)}), bf16[2048,2048]{1,0:T(8,128)(2,1)}) %reduce-scatter.29.cloned.1.call-update) | async-done | bytes 8388624
  2204.7 18.0 fusion.52
  2253.0 28.0 %all-reduce.10 = (bf16[512]{0:T(512)(128)(2,1)S(1)}, bf16[512]{0:T(512)(128)(2,1)S(1)}, bf16[512]{0:T(512)(128)(2,1)S(1)}, bf16[512]{0:T(512)(128)(2,1)S(1)}, bf...) all-reduce(bf16[512]{0:T(512)(128)(2,1)S(1)} %dynamic-slice.1, ...), channel_id=1, replica_groups=mesh['replica'=8,'group'=4] {'replica'}, use_global_device_ids=true, to_apply=%region_19.20 | all-reduce | flops 6144 | bytes 24576 | tf_op jit(solution)/shard_map/psum | solution.py:326
  2287.5 397.6 %all-reduce.15.cloned.1.call-done = (bf16[512,2048]{1,0:T(8,128)(2,1)}, bf16[512,2048]{1,0:T(8,128)(2,1)}, bf16[512,2048]{1,0:T(8,128)(2,1)}, bf16[512,2048]{1,0...) async-done(((bf16[512,2048]{1,0:T(8,128)(2,1)}, bf16[512,2048]{1,0:T(8,128)(2,1)}, bf16[512,2048]{1,0:T(8,128)(2,1)}, bf16[512,2048]{1,0:T(8,128)(2,1)}, ...) | async-done | bytes 25165840 | tf_op jit(solution)/shard_map/psum | solution.py:328
  (295 shorter events, 321.4 us)
Async XLA Ops:
  7.2 93.1 %all-gather.17.cloned.1.call-start = ((), (), s32[]{:S(2)}) async-start(), calls=%async_computation.9 | async-start | bytes 10485760 | tf_op jit(solution)/shard_map/all_gather | solution.py:116
  8.0 181.9 %all-gather.23.cloned.1.call-start = ((), (), s32[]{:S(2)}) async-start(), calls=%async_computation.12 | async-start | bytes 10485760 | tf_op jit(solution)/shard_map/all_gather | solution.py:115
  8.7 364.2 %all-gather.21.cloned.1.call-start = ((), (), s32[]{:S(2)}) async-start(), calls=%async_computation.11 | async-start | bytes 10485760 | tf_op jit(solution)/shard_map/all_gather | solution.py:114
  9.4 390.0 %all-gather.19.cloned.1.call-start = ((), (), s32[]{:S(2)}) async-start(), calls=%async_computation.10 | async-start | bytes 2621440 | tf_op jit(solution)/shard_map/all_gather | solution.py:136
  105.9 331.2 %all-gather.25.cloned.1.call-start = ((), (), s32[]{:S(2)}) async-start(), calls=%async_computation.13 | async-start | bytes 2621440 | tf_op jit(solution)/shard_map/all_gather | solution.py:135
  195.4 540.7 %all-gather.27.cloned.1.call-start = ((), (), s32[]{:S(2)}) async-start(), calls=%async_computation.14 | async-start | bytes 41943040 | tf_op jit(solution)/shard_map/all_gather | solution.py:162
  195.9 839.2 %all-gather.29.cloned.1.call-start = ((), (), s32[]{:S(2)}) async-start(), calls=%async_computation.15 | async-start | bytes 41943040 | tf_op jit(solution)/shard_map/all_gather | solution.py:164
  202.8 138.7 %copy-start.26 = (bf16[512]{0:T(512)(128)(2,1)S(1)}, bf16[512]{0:T(512)(128)(2,1)}, u32[]{:S(2)}) copy-start(bf16[512]{0:T(512)(128)(2,1)} %param.29) | copy-start | bytes 3076
  202.8 147.5 %copy-start.21 = (bf16[2048]{0:T(1024)(128)(2,1)S(1)}, bf16[2048]{0:T(1024)(128)(2,1)}, u32[]{:S(2)}) copy-start(bf16[2048]{0:T(1024)(128)(2,1)} %param.38) | copy-start | bytes 12292
  202.8 154.9 %copy-start.27 = (bf16[512]{0:T(512)(128)(2,1)S(1)}, bf16[512]{0:T(512)(128)(2,1)}, u32[]{:S(2)}) copy-start(bf16[512]{0:T(512)(128)(2,1)} %param.36) | copy-start | bytes 3076
  202.8 163.0 %copy-start.28 = (bf16[512]{0:T(512)(128)(2,1)S(1)}, bf16[512]{0:T(512)(128)(2,1)}, u32[]{:S(2)}) copy-start(bf16[512]{0:T(512)(128)(2,1)} %param.35) | copy-start | bytes 3076
  202.8 170.1 %copy-start.30 = (s32[128]{0:T(128)S(1)}, s32[128]{0:T(128)}, u32[]{:S(2)}) copy-start(s32[128]{0:T(128)} %param.25) | copy-start | bytes 1540
  202.8 254.0 %all-to-all-start = ((bf16[4,512,2048]{2,1,0:T(8,128)(2,1)}), bf16[4,512,2048]{2,1,0:T(8,128)(2,1)}, u32[]{:S(2)}, u32[]{:S(2)}) async-start(bf16[4,512,2048]{2,1,0:T(8,128)(2,1)} %stack.2), calls=%async_computation | async-start | bytes 16777216 | tf_op jit(solution)/shard_map/all_to_all | solution.py:118
  208.6 916.0 %all-gather.31.cloned.1.call-start = ((), (), s32[]{:S(2)}) async-start(), calls=%async_computation.16 | async-start | bytes 10485760 | tf_op jit(solution)/shard_map/all_gather | solution.py:177
  209.4 996.0 %reduce-scatter.25.cloned.1.call-start = ((), (), s32[]{:S(2)}) async-start(), calls=%async_computation.22 | async-start | bytes 2621440
  1170.0 74.2 %reduce-scatter.27.cloned.1.call-start = ((), (), s32[]{:S(2)}) async-start(), calls=%async_computation.23 | async-start | bytes 2621440
  1174.1 160.3 %reduce-scatter.15.cloned.1.call-start = ((), (), s32[]{:S(2)}) async-start(), calls=%async_computation.17 | async-start | bytes 10485760 | tf_op jit(solution)/shard_map/reduce_scatter | solution.py:291
  1180.0 244.0 %reduce-scatter.21.cloned.1.call-start = ((), (), s32[]{:S(2)}) async-start(), calls=%async_computation.20 | async-start | bytes 10485760 | tf_op jit(solution)/shard_map/reduce_scatter | solution.py:309
  1186.8 327.3 %reduce-scatter.17.cloned.1.call-start = ((), (), s32[]{:S(2)}) async-start(), calls=%async_computation.18 | async-start | bytes 10485760 | tf_op jit(solution)/shard_map/reduce_scatter | solution.py:297
  1212.3 391.4 %reduce-scatter.19.cloned.1.call-start = ((), (), s32[]{:S(2)}) async-start(), calls=%async_computation.19 | async-start | bytes 10485760 | tf_op jit(solution)/shard_map/reduce_scatter | solution.py:303
  1251.1 644.2 %reduce-scatter.23.cloned.1.call-start = ((), (), s32[]{:S(2)}) async-start(), calls=%async_computation.21 | async-start | bytes 41943040 | tf_op jit(solution)/shard_map/reduce_scatter | solution.py:189
  1268.0 919.2 %reduce-scatter.29.cloned.1.call-start = ((), (), s32[]{:S(2)}) async-start(), calls=%async_computation.24 | async-start | bytes 41943040
  1285.5 1399.5 %all-reduce.15.cloned.1.call-start = ((), (), s32[]{:S(2)}) async-start(), calls=%async_computation.25 | async-start | bytes 50331648 | tf_op jit(solution)/shard_map/psum | solution.py:328
  2229.3 56.9 %copy-start.12 = (f32[128,2048]{1,0:T(8,128)S(1)}, f32[128,2048]{1,0:T(8,128)}, u32[]{:S(2)}) copy-start(f32[128,2048]{1,0:T(8,128)} %get-tuple-element.224) | copy-start | bytes 3145732
  (50 other events, 170.8 us)
Sparse Core Ops, SparseCore 0:
  9.9 90.3 all-gather.16
  102.2 87.5 all-gather.22
  191.7 170.0 all-gather.20
  364.1 35.3 all-gather.18
  401.7 35.2 all-gather.24
  438.8 297.2 all-gather.26
  737.9 297.2 all-gather.28
  1036.9 87.5 all-gather.30
  1170.1 35.1 reduce-scatter.24
  1209.0 35.1 reduce-scatter.26
  1247.9 86.3 reduce-scatter.14
  1337.6 86.4 reduce-scatter.20
  1427.6 86.3 reduce-scatter.16
  1517.3 86.4 reduce-scatter.18
  1606.6 288.6 reduce-scatter.22
  1898.5 288.6 reduce-scatter.28
  2190.3 494.6 all-reduce.14
